TPU v7x, 32 devices: a whole 2x2x4 slice. The times are simulated.
32 devices in a mesh: gx: 8 (over y, x, core), gy: 4 (over z).
Axes of the slice: x: 2, y: 2, z: 4, core: 2. Of those that a mesh axis runs over, the one named last changes fastest.
Arguments:
- tokens: bfloat16 [3072, 2048], P('gx', 'gy'), may hold values from -40 to 40
- gain: float32 [2048], replicated, may hold values from 0.1 to 1.9
- w_qkv: bfloat16 [2048, 3, 16, 128], P('gx', None, 'gy'), may hold values from -0.176776695 to 0.176776695
- w_out: bfloat16 [2048, 2048], P('gx', 'gy'), may hold values from -0.125 to 0.125
- lengths: int32 [6], replicated, may hold values from 1 to 2048, 3072 in all
Outputs:
- mixed: bfloat16 [3072, 2048], P('gx', 'gy')
- key_cache: bfloat16 [3072, 16, 128], P('gx', 'gy')
- value_cache: bfloat16 [3072, 16, 128], P('gx', 'gy')
Inputs may be any that keep to these rules, and one draw needn't show every extreme that they name: lengths are positive and sum to 3072; the longest is exactly 2048.
All inputs are finite; a program needn't handle non-finite values.
Results may differ from a plain program's by a relative error of at most 0.012.
The roundings to bfloat16 on the way count: a program that leaves them out, or rounds other values in their place, can miss the bound.
Values may be sent and summed in bfloat16 or wider, within the bound.
No kernel may reach another device: no remote copies, remote signals or barrier semaphores. Data moves between devices by JAX's collectives and lax.ppermute only.
A program may use at most 64 MiB of HBM per device.

v0:
```python
import math
import jax
import jax.numpy as jnp
from jax import lax
from jax.sharding import PartitionSpec as P


def rotate(vectors, position):
    half = vectors.shape[-1] // 2
    freq = 10000.0 ** (-(2.0 * jnp.arange(half, dtype=jnp.float32)) / vectors.shape[-1])
    angle = position.astype(jnp.float32)[:, None, None] * freq[None, None, :]
    cosine = jnp.cos(angle)
    sine = jnp.sin(angle)
    first = vectors[..., :half]
    second = vectors[..., half:]
    return jnp.concatenate(
        [first * cosine - second * sine, second * cosine + first * sine], axis=-1
    )


def block_rows(count):
    size = count
    while size > 1024 and size % 2 == 0:
        size = size // 2
    return size


def local(tokens, gain, w_qkv, w_out, lengths):
    tok_dev = tokens.shape[0]
    hloc = w_qkv.shape[2]
    hsize = w_qkv.shape[3]
    whole = lax.all_gather(tokens, "gy", axis=1, tiled=True)
    wide = whole.astype(jnp.float32)
    meansq = jnp.mean(wide * wide, axis=-1, keepdims=True)
    normed = (wide * lax.rsqrt(meansq + 1e-06) * gain[None, :]).astype(jnp.bfloat16)
    piece = lax.all_gather(w_qkv, "gx", axis=0, tiled=True)
    columns = normed
    projected = jnp.dot(
        columns, piece.reshape(piece.shape[0], -1), preferred_element_type=jnp.float32
    )
    projected = projected.reshape(tok_dev, 3, hloc, hsize)
    mine = lax.axis_index("gx")
    glob = mine * tok_dev + jnp.arange(tok_dev, dtype=jnp.int32)
    doc_start = jnp.cumsum(lengths) - lengths
    begin = jnp.max(jnp.where(doc_start[None, :] <= glob[:, None], doc_start[None, :], 0), axis=1)
    position = glob - begin
    query = rotate(projected[:, 0], position).astype(jnp.bfloat16)
    keys_own = rotate(projected[:, 1], position).astype(jnp.bfloat16)
    vals_own = projected[:, 2].astype(jnp.bfloat16)
    scale = 1.0 / math.sqrt(hsize)

    def tile_step(state, keys_blk, vals_blk, first):
        running, totals, accum = state
        kidx = first + jnp.arange(keys_blk.shape[0], dtype=jnp.int32)
        score = (
            jnp.einsum("qhd,khd->hqk", query, keys_blk, preferred_element_type=jnp.float32) * scale
        )
        keep = (kidx[None, :] >= begin[:, None]) & (kidx[None, :] <= glob[:, None])
        score = jnp.where(keep[None], score, -1e30)
        newmax = jnp.maximum(running, jnp.max(score, axis=-1))
        weight = jnp.where(keep[None], jnp.exp(score - newmax[..., None]), 0.0)
        factor = jnp.exp(running - newmax)
        totals = totals * factor + jnp.sum(weight, axis=-1)
        update = jnp.einsum(
            "hqk,khd->hqd",
            weight.astype(jnp.bfloat16),
            vals_blk,
            preferred_element_type=jnp.float32,
        )
        accum = accum * factor[..., None] + update
        return (newmax, totals, accum)

    initial = (
        jnp.full((hloc, tok_dev), -1e30, jnp.float32),
        jnp.zeros((hloc, tok_dev), jnp.float32),
        jnp.zeros((hloc, tok_dev, hsize), jnp.float32),
    )
    keys_piece = lax.all_gather(keys_own, "gx", axis=0, tiled=True)
    vals_piece = lax.all_gather(vals_own, "gx", axis=0, tiled=True)
    count = keys_piece.shape[0]
    size = block_rows(count)

    def one_tile(number, inner):
        first = (number * size).astype(jnp.int32)
        keys_blk = lax.dynamic_slice_in_dim(keys_piece, first, size, 0)
        vals_blk = lax.dynamic_slice_in_dim(vals_piece, first, size, 0)
        return tile_step(inner, keys_blk, vals_blk, first)

    running, totals, accum = lax.fori_loop(0, count // size, one_tile, initial)
    attended = (accum / totals[..., None]).astype(jnp.bfloat16)
    attended = jnp.transpose(attended, (1, 0, 2)).reshape(tok_dev, hloc * hsize)
    all_heads = lax.all_gather(attended, "gy", axis=1, tiled=True)
    columns = all_heads
    mixed = jnp.dot(
        columns, lax.all_gather(w_out, "gx", axis=0, tiled=True), preferred_element_type=jnp.float32
    ).astype(jnp.bfloat16)
    return (mixed, keys_own, vals_own)


def solution(mesh):
    return jax.shard_map(
        local,
        mesh=mesh,
        in_specs=(P("gx", "gy"), P(), P("gx", None, "gy", None), P("gx", "gy"), P()),
        out_specs=(P("gx", "gy"), P("gx", "gy", None), P("gx", "gy", None)),
        check_vma=False,
    )
```

profile of v0, /device:TPU:0, one launch (start us, length us, event | category | flops | bytes accessed | tf_op | source)
XLA Modules:
  0.0 282.4 jit_solution(10697021689812042305)
XLA Ops:
  7.2 0.0 all-gather.8.cloned.1.call-start
  7.2 0.7 all-gather.8.cloned.1.call-update
  7.9 0.0 all-gather.10.cloned.1.call-start
  7.9 0.7 all-gather.10.cloned.1.call-update
  8.6 0.0 all-gather.12.cloned.1.call-start
  8.7 0.8 reduce-window.9
  9.5 0.7 bitcast_subtract_fusion
  10.2 0.1 select_reduce_fusion
  10.3 0.4 multiply_cosine_fusion
  10.7 38.7 %all-gather.8.cloned.1.call-done = bf16[384,2048]{1,0:T(8,128)(2,1)} async-done(((bf16[384,512]{1,0:T(8,128)(2,1)}), bf16[384,2048]{1,0:T(8,128)(2,1)}) %all-gather.8.cloned.1.call-update) | async-done | bytes 1572880 | tf_op jit(solution)/shard_map/all_gather | solution.py:32
  49.4 1.8 fusion.22
  51.2 0.0 copy-start.2
  51.2 44.5 %all-gather.10.cloned.1.call-done = bf16[2048,3,4,128]{3,2,1,0:T(4,128)(2,1)} async-done(((bf16[256,3,4,128]{3,2,1,0:T(4,128)(2,1)}), bf16[2048,3,4,128]{3,2,1,0:T(4,128)(2,1)}) %all-gather.10.cloned.1.call-update) | async-done | bytes 6291472 | tf_op jit(solution)/shard_map/all_gather | solution.py:36
  95.7 10.6 %copy.41 = bf16[2048,3,4,128]{0,3,2,1:T(8,128)(2,1)} copy(bf16[2048,3,4,128]{3,2,1,0:T(4,128)(2,1)} %all-gather.10.cloned.1.call-done) | data formatting | bytes 12582912 | tf_op jit(solution)/shard_map/reshape | solution.py:39
  106.3 0.0 copy-done.2
  106.3 6.2 %fusion.20 = f32[384,3,4,128]{0,3,2,1:T(8,128)S(1)} fusion(bf16[2048,3,4,128]{0,3,2,1:T(8,128)(2,1)} %copy.41, bf16[384,2048]{1,0:T(8,128)(2,1)} %all-gather.8.cloned.1.call-done, f32[2048]{0:T(1024)S(1)} %copy-done.2, f32[384]{0:T(512)S(1)} %add_rsqrt_fusion), kind=kOutput, calls=%fused_computation.25 | convolution fusion | flops 2419064832 | bytes 10233344 | tf_op jit(solution)/shard_map/dot_general | solution.py:38
  112.5 0.1 slice_bitcast_fusion
  112.6 0.2 subtract_convert_fusion
  112.8 0.8 pad_maximum_fusion
  113.6 0.0 all-gather.12.cloned.1.call-update
  113.6 0.0 all-gather.18.cloned.1.call-start
  113.7 0.8 slice.47
  114.5 0.0 all-gather.18.cloned.1.call-update
  114.5 0.0 all-gather.16.cloned.1.call-start
  114.6 0.5 all-gather.16.cloned.1.call-update
  115.1 0.0 all-gather.14.cloned.1.call-start
  115.2 0.2 copy.34
  115.5 31.2 %all-gather.12.cloned.1.call-done = bf16[3072,4,128]{0,2,1:T(8,128)(2,1)} async-done(((bf16[384,4,128]{0,2,1:T(8,128)(2,1)}), bf16[3072,4,128]{0,2,1:T(8,128)(2,1)}) %all-gather.12.cloned.1.call-update) | async-done | bytes 3145744 | tf_op jit(solution)/shard_map/all_gather | solution.py:78
  146.6 35.1 %all-gather.18.cloned.1.call-done = bf16[3072,1,4,128]{0,3,2,1:T(8,128)(2,1)} async-done(((bf16[384,1,4,128]{0,3,2,1:T(8,128)(2,1)}), bf16[3072,1,4,128]{0,3,2,1:T(8,128)(2,1)}) %all-gather.18.cloned.1.call-update) | async-done | bytes 3145744 | tf_op jit(solution)/shard_map/all_gather | solution.py:79
  181.8 50.4 %while.18 = (s32[]{:T(128)}, f32[4,384]{1,0:T(4,128)S(1)}, f32[4,384]{1,0:T(4,128)S(1)}, f32[4,384,128]{2,1,0:T(8,128)}, s32[384]{0:T(512)S(1)}, /*index=5*/bf16...) while((s32[]{:T(128)}, f32[4,384]{1,0:T(4,128)S(1)}, ...), condition=%wide.region_6.7_spmd.clone, body=%wide.region_3.6_spmd.clone.sunk | while | flops 620798592 | bytes 37858016 | solution.py:89
  181.8 0.3 compare_and_fusion.2
  182.1 4.4 %fusion.42 = (f32[4,384]{1,0:T(4,128)S(1)}, f32[4,768,384]{2,1,0:T(8,128)}) fusion(pred[384,768]{0,1:T(8,128)(4,1)S(1)} %compare_and_fusion.2, bf16[384,4,128]{2,0,1:T(8,128)(2,1)S(1)} %get-tuple-element.368, bf16[3072,4,128]{0,2,1:T(8,128)(2,1)} %get-tuple-element.367, s32[]{:T(128)S(6)} %select_n.63), kind=kOutput, calls=%fused_computation.3.clone.1 | convolution fusion | flops 305527296 | bytes 6199300 | tf_op jit(solution)/shard_map/while/body/eval_jaxpr/qhd,khd->hqk/dot_general | solution.py:56
  186.5 0.0 copy-start
  186.5 3.7 %fusion.43 = f32[4,384]{1,0:T(4,128)S(1)} fusion(f32[4,768,384]{2,1,0:T(8,128)} %get-tuple-element.333, f32[4,384]{1,0:T(4,128)S(1)} %select_maximum_fusion.2, pred[384,768]{0,1:T(8,128)(4,1)S(1)} %compare_and_fusion.2), kind=kLoop, calls=%fused_computation.5.clone.1 | loop fusion | flops 5896704 | bytes 5025792 | tf_op jit(solution)/shard_map/while/body/eval_jaxpr/reduce_sum | solution.py:63
  190.2 0.1 copy-done
  190.3 3.9 %fusion.45 = f32[4,384,128]{2,1,0:T(8,128)} fusion(f32[4,768,384]{2,1,0:T(8,128)S(1)} %copy-done, f32[4,384]{1,0:T(4,128)S(1)} %select_maximum_fusion.2, pred[384,768]{0,1:T(8,128)(4,1)S(1)} %compare_and_fusion.2, f32[4,384,128]{2,1,0:T(8,128)} %get-tuple-element.352, bf16[3072,4,128]{0,2,1:T(8,128)(2,1)} %get-tuple-element.369, s32[]{:T(128)S(6)} %select_n.63, ...), kind=kOutput, calls=%fused_computation.8.clone.1 | convolution fusion | flops 308477952 | bytes 7385093 | tf_op jit(solution)/shard_map/while/body/eval_jaxpr/hqk,khd->hqd/dot_general | solution.py:64
  194.2 0.3 compare_and_fusion.2
  194.5 4.4 %fusion.42 = (f32[4,384]{1,0:T(4,128)S(1)}, f32[4,768,384]{2,1,0:T(8,128)}) fusion(pred[384,768]{0,1:T(8,128)(4,1)S(1)} %compare_and_fusion.2, bf16[384,4,128]{2,0,1:T(8,128)(2,1)S(1)} %get-tuple-element.368, bf16[3072,4,128]{0,2,1:T(8,128)(2,1)} %get-tuple-element.367, s32[]{:T(128)S(6)} %select_n.63), kind=kOutput, calls=%fused_computation.3.clone.1 | convolution fusion | flops 305527296 | bytes 6199300 | tf_op jit(solution)/shard_map/while/body/eval_jaxpr/qhd,khd->hqk/dot_general | solution.py:56
  198.9 0.0 copy-start
  198.9 3.7 %fusion.43 = f32[4,384]{1,0:T(4,128)S(1)} fusion(f32[4,768,384]{2,1,0:T(8,128)} %get-tuple-element.333, f32[4,384]{1,0:T(4,128)S(1)} %select_maximum_fusion.2, pred[384,768]{0,1:T(8,128)(4,1)S(1)} %compare_and_fusion.2), kind=kLoop, calls=%fused_computation.5.clone.1 | loop fusion | flops 5896704 | bytes 5025792 | tf_op jit(solution)/shard_map/while/body/eval_jaxpr/reduce_sum | solution.py:63
  202.6 0.4 copy-done
  203.0 4.1 %fusion.45 = f32[4,384,128]{2,1,0:T(8,128)} fusion(f32[4,768,384]{2,1,0:T(8,128)S(1)} %copy-done, f32[4,384]{1,0:T(4,128)S(1)} %select_maximum_fusion.2, pred[384,768]{0,1:T(8,128)(4,1)S(1)} %compare_and_fusion.2, f32[4,384,128]{2,1,0:T(8,128)} %get-tuple-element.352, bf16[3072,4,128]{0,2,1:T(8,128)(2,1)} %get-tuple-element.369, s32[]{:T(128)S(6)} %select_n.63, ...), kind=kOutput, calls=%fused_computation.8.clone.1 | convolution fusion | flops 308477952 | bytes 7385093 | tf_op jit(solution)/shard_map/while/body/eval_jaxpr/hqk,khd->hqd/dot_general | solution.py:64
  207.1 0.3 compare_and_fusion.2
  207.4 4.4 %fusion.42 = (f32[4,384]{1,0:T(4,128)S(1)}, f32[4,768,384]{2,1,0:T(8,128)}) fusion(pred[384,768]{0,1:T(8,128)(4,1)S(1)} %compare_and_fusion.2, bf16[384,4,128]{2,0,1:T(8,128)(2,1)S(1)} %get-tuple-element.368, bf16[3072,4,128]{0,2,1:T(8,128)(2,1)} %get-tuple-element.367, s32[]{:T(128)S(6)} %select_n.63), kind=kOutput, calls=%fused_computation.3.clone.1 | convolution fusion | flops 305527296 | bytes 6199300 | tf_op jit(solution)/shard_map/while/body/eval_jaxpr/qhd,khd->hqk/dot_general | solution.py:56
  211.8 0.0 copy-start
  211.8 3.7 %fusion.43 = f32[4,384]{1,0:T(4,128)S(1)} fusion(f32[4,768,384]{2,1,0:T(8,128)} %get-tuple-element.333, f32[4,384]{1,0:T(4,128)S(1)} %select_maximum_fusion.2, pred[384,768]{0,1:T(8,128)(4,1)S(1)} %compare_and_fusion.2), kind=kLoop, calls=%fused_computation.5.clone.1 | loop fusion | flops 5896704 | bytes 5025792 | tf_op jit(solution)/shard_map/while/body/eval_jaxpr/reduce_sum | solution.py:63
  215.5 0.1 copy-done
  215.6 4.1 %fusion.45 = f32[4,384,128]{2,1,0:T(8,128)} fusion(f32[4,768,384]{2,1,0:T(8,128)S(1)} %copy-done, f32[4,384]{1,0:T(4,128)S(1)} %select_maximum_fusion.2, pred[384,768]{0,1:T(8,128)(4,1)S(1)} %compare_and_fusion.2, f32[4,384,128]{2,1,0:T(8,128)} %get-tuple-element.352, bf16[3072,4,128]{0,2,1:T(8,128)(2,1)} %get-tuple-element.369, s32[]{:T(128)S(6)} %select_n.63, ...), kind=kOutput, calls=%fused_computation.8.clone.1 | convolution fusion | flops 308477952 | bytes 7385093 | tf_op jit(solution)/shard_map/while/body/eval_jaxpr/hqk,khd->hqd/dot_general | solution.py:64
  219.7 0.3 compare_and_fusion.2
  220.0 4.4 %fusion.42 = (f32[4,384]{1,0:T(4,128)S(1)}, f32[4,768,384]{2,1,0:T(8,128)}) fusion(pred[384,768]{0,1:T(8,128)(4,1)S(1)} %compare_and_fusion.2, bf16[384,4,128]{2,0,1:T(8,128)(2,1)S(1)} %get-tuple-element.368, bf16[3072,4,128]{0,2,1:T(8,128)(2,1)} %get-tuple-element.367, s32[]{:T(128)S(6)} %select_n.63), kind=kOutput, calls=%fused_computation.3.clone.1 | convolution fusion | flops 305527296 | bytes 6199300 | tf_op jit(solution)/shard_map/while/body/eval_jaxpr/qhd,khd->hqk/dot_general | solution.py:56
  224.4 0.0 copy-start
  224.4 3.7 %fusion.43 = f32[4,384]{1,0:T(4,128)S(1)} fusion(f32[4,768,384]{2,1,0:T(8,128)} %get-tuple-element.333, f32[4,384]{1,0:T(4,128)S(1)} %select_maximum_fusion.2, pred[384,768]{0,1:T(8,128)(4,1)S(1)} %compare_and_fusion.2), kind=kLoop, calls=%fused_computation.5.clone.1 | loop fusion | flops 5896704 | bytes 5025792 | tf_op jit(solution)/shard_map/while/body/eval_jaxpr/reduce_sum | solution.py:63
  228.1 0.1 copy-done
  228.1 4.1 %fusion.45 = f32[4,384,128]{2,1,0:T(8,128)} fusion(f32[4,768,384]{2,1,0:T(8,128)S(1)} %copy-done, f32[4,384]{1,0:T(4,128)S(1)} %select_maximum_fusion.2, pred[384,768]{0,1:T(8,128)(4,1)S(1)} %compare_and_fusion.2, f32[4,384,128]{2,1,0:T(8,128)} %get-tuple-element.352, bf16[3072,4,128]{0,2,1:T(8,128)(2,1)} %get-tuple-element.369, s32[]{:T(128)S(6)} %select_n.63, ...), kind=kOutput, calls=%fused_computation.8.clone.1 | convolution fusion | flops 308477952 | bytes 7385093 | tf_op jit(solution)/shard_map/while/body/eval_jaxpr/hqk,khd->hqd/dot_general | solution.py:64
  232.2 0.0 copy-start.1
  232.2 1.4 copy.36
  233.7 0.8 divide_convert_fusion
  234.5 0.0 all-gather.14.cloned.1.call-update
  234.5 0.0 copy-done.1
  234.5 1.0 copy.37
  235.5 1.0 copy.38
  236.5 0.0 all-gather.16.cloned.1.call-done
  236.5 35.2 %all-gather.14.cloned.1.call-done = bf16[384,2048]{0,1:T(8,128)(2,1)} async-done(((bf16[384,512]{0,1:T(8,128)(2,1)}), bf16[384,2048]{0,1:T(8,128)(2,1)}) %all-gather.14.cloned.1.call-update) | async-done | bytes 1572880 | tf_op jit(solution)/shard_map/all_gather | solution.py:92
  271.7 3.8 %convolution_convert_fusion = bf16[384,512]{1,0:T(8,128)(2,1)} fusion(bf16[384,2048]{0,1:T(8,128)(2,1)} %all-gather.14.cloned.1.call-done, bf16[2048,512]{1,0:T(8,128)(2,1)} %all-gather.16.cloned.1.call-done), kind=kOutput, calls=%fused_computation.35 | convolution fusion | flops 805502976 | bytes 4063232 | tf_op jit(solution)/shard_map/dot_general | solution.py:94
  (29 shorter events, 0.3 us)
Async XLA Ops:
  7.2 42.2 %all-gather.8.cloned.1.call-start = ((), (), s32[]{:S(2)}) async-start(), calls=%async_computation | async-start | bytes 1966080 | tf_op jit(solution)/shard_map/all_gather | solution.py:32
  7.9 87.8 %all-gather.10.cloned.1.call-start = ((), (), s32[]{:S(2)}) async-start(), calls=%async_computation.1 | async-start | bytes 7077888 | tf_op jit(solution)/shard_map/all_gather | solution.py:36
  8.6 138.0 %all-gather.12.cloned.1.call-start = ((), (), s32[]{:S(2)}) async-start(), calls=%async_computation.2 | async-start | bytes 3538944 | tf_op jit(solution)/shard_map/all_gather | solution.py:78
  51.2 55.1 %copy-start.2 = (f32[2048]{0:T(1024)S(1)}, f32[2048]{0:T(1024)}, u32[]{:S(2)}) copy-start(f32[2048]{0:T(1024)} %param.8) | copy-start | bytes 24580
  113.6 68.1 %all-gather.18.cloned.1.call-start = ((), (), s32[]{:S(2)}) async-start(), calls=%async_computation.5 | async-start | bytes 3538944 | tf_op jit(solution)/shard_map/all_gather | solution.py:79
  114.5 122.0 %all-gather.16.cloned.1.call-start = ((), (), s32[]{:S(2)}) async-start(), calls=%async_computation.4 | async-start | bytes 2359296 | tf_op jit(solution)/shard_map/all_gather | solution.py:95
  115.1 156.6 %all-gather.14.cloned.1.call-start = ((), (), s32[]{:S(2)}) async-start(), calls=%async_computation.3 | async-start | bytes 1966080 | tf_op jit(solution)/shard_map/all_gather | solution.py:92
  186.5 3.8 %copy-start = (f32[4,768,384]{2,1,0:T(8,128)S(1)}, f32[4,768,384]{2,1,0:T(8,128)}, u32[]{:S(2)}) copy-start(f32[4,768,384]{2,1,0:T(8,128)} %get-tuple-element.333) | copy-start | bytes 14155780 | tf_op jit(solution)/shard_map/while
  198.9 4.1 %copy-start = (f32[4,768,384]{2,1,0:T(8,128)S(1)}, f32[4,768,384]{2,1,0:T(8,128)}, u32[]{:S(2)}) copy-start(f32[4,768,384]{2,1,0:T(8,128)} %get-tuple-element.333) | copy-start | bytes 14155780 | tf_op jit(solution)/shard_map/while
  211.8 3.8 %copy-start = (f32[4,768,384]{2,1,0:T(8,128)S(1)}, f32[4,768,384]{2,1,0:T(8,128)}, u32[]{:S(2)}) copy-start(f32[4,768,384]{2,1,0:T(8,128)} %get-tuple-element.333) | copy-start | bytes 14155780 | tf_op jit(solution)/shard_map/while
  224.4 3.8 %copy-start = (f32[4,768,384]{2,1,0:T(8,128)S(1)}, f32[4,768,384]{2,1,0:T(8,128)}, u32[]{:S(2)}) copy-start(f32[4,768,384]{2,1,0:T(8,128)} %get-tuple-element.333) | copy-start | bytes 14155780 | tf_op jit(solution)/shard_map/while
  232.2 2.3 copy-start.1
Sparse Core Ops, SparseCore 0:
  9.6 39.7 all-gather.7
  51.3 44.3 all-gather.9
  113.8 32.8 all-gather.11
  148.9 32.8 all-gather.17
  183.5 27.8 all-gather.15
  234.6 37.0 all-gather.13
where the time goes:
time: 283 us; the launch traced here: 282 us
  waiting for transfers between devices  187 us (66%)
  matrix products  43.8 us (15%)
  other arithmetic  21.6 us (8%)
  local copies, waits for them, and re-layouts  15.8 us (6%)
  between operations  14.2 us (5%)
    all_gather x1, waiting for transfers between devices, local(): piece = lax.all_gather(w_qkv, 'gx', axis=0, tiled=True)  44.5 us
    all_gather x1, waiting for transfers between devices, local(): whole = lax.all_gather(tokens, 'gy', axis=1, tiled=True)  38.7 us
    all_gather x1, waiting for transfers between devices, local(): all_heads = lax.all_gather(attended, 'gy', axis=1, tiled=True)  35.2 us
    all_gather x1, waiting for transfers between devices, local(): vals_piece = lax.all_gather(vals_own, 'gx', axis=0, tiled=True)  35.1 us
    all_gather x1, waiting for transfers between devices, local(): keys_piece = lax.all_gather(keys_own, 'gx', axis=0, tiled=True)  31.2 us
    dot_general x4, matrix products, tile_step(): jnp.einsum('qhd,khd->hqk', query, keys_blk, preferred_element_type=jnp.fl...  17.7 us
    dot_general x4, matrix products, tile_step(): jnp.einsum('hqk,khd->hqd', weight.astype(jnp.bfloat16), vals_blk, preferr...  16.1 us
    reduce_sum x4, other arithmetic, tile_step(): totals = totals * factor + jnp.sum(weight, axis=-1)  14.6 us
  transfers between devices with their start and end apart: 6, of which 5 were waited for; matrix products, arithmetic and copies ran while one was open for 21% of the time, Pallas kernels for 0%

commit v1 on v0

--- a/solution.py
+++ b/solution.py
@@ -29,7 +29,17 @@
     tok_dev = tokens.shape[0]
     hloc = w_qkv.shape[2]
     hsize = w_qkv.shape[3]
-    whole = lax.all_gather(tokens, "gy", axis=1, tiled=True)
+    e_now = lax.axis_size("gy")
+    o_now = lax.axis_index("gy")
+    v_next, frame_out, oldest = (e_now, o_now, tokens.shape[1])
+    views = [(dd, (dd + 1) % v_next) for dd in range(v_next)]
+    whole = jnp.zeros((*tokens.shape[:1], v_next * oldest, *tokens.shape[2:]), tokens.dtype)
+    piece_next = tokens
+    for b in range(v_next):
+        carry = (frame_out - b) % v_next
+        whole = lax.dynamic_update_slice_in_dim(whole, piece_next, carry * oldest, axis=1)
+        if b < v_next - 1:
+            piece_next = lax.ppermute(piece_next, "gy", views)
     wide = whole.astype(jnp.float32)
     meansq = jnp.mean(wide * wide, axis=-1, keepdims=True)
     normed = (wide * lax.rsqrt(meansq + 1e-06) * gain[None, :]).astype(jnp.bfloat16)

time: 283 us -> 241 us (0.85)
  waiting for transfers between devices: 187 us -> 144 us
  matrix products: 43.8 us -> 39.8 us
  local copies, waits for them, and re-layouts: 15.8 us -> 19.1 us
  starting transfers between devices: 0.24 us -> 3.28 us
    all_gather x1 -> x0, waiting for transfers between devices: 38.7 us -> none  [local(): whole = lax.all_gather(tokens, 'gy', axis=1, tiled=True)]
    all_gather x1, waiting for transfers between devices: 44.5 us -> 12 us  [local(): piece = lax.all_gather(w_qkv, 'gx', axis=0, tiled=True)]
    ppermute x0 -> x3, waiting for transfers between devices: none -> 31.2 us  [local(): piece_next = lax.ppermute(piece_next, 'gy', views)]
    dot_general x4, matrix products: 16.1 us -> 12.6 us  [tile_step(): jnp.einsum('hqk,khd->hqd', weight.astype(jnp.bfloat16), vals_blk, preferr...]
    ppermute x0 -> x3, starting transfers between devices: none -> 3.08 us  [local(): piece_next = lax.ppermute(piece_next, 'gy', views)]
  transfers between devices with their start and end apart: 6 -> 8, of which waited for: 5 -> 7; matrix products, arithmetic and copies ran while one was open for 21% -> 23% of each run, Pallas kernels for 0% -> 0%
where the time goes in v1:
time: 241 us
  waiting for transfers between devices  144 us (60%)
  matrix products  39.8 us (17%)
  other arithmetic  20.2 us (8%)
  local copies, waits for them, and re-layouts  19.1 us (8%)
  between operations  14 us (6%)
  starting transfers between devices  3.28 us (1%)
    all_gather x1, waiting for transfers between devices, local(): vals_piece = lax.all_gather(vals_own, 'gx', axis=0, tiled=True)  35.3 us
    all_gather x1, waiting for transfers between devices, local(): all_heads = lax.all_gather(attended, 'gy', axis=1, tiled=True)  34.2 us
    ppermute x3, waiting for transfers between devices, local(): piece_next = lax.ppermute(piece_next, 'gy', views)  31.2 us
    all_gather x1, waiting for transfers between devices, local(): keys_piece = lax.all_gather(keys_own, 'gx', axis=0, tiled=True)  30 us
    dot_general x4, matrix products, tile_step(): jnp.einsum('qhd,khd->hqk', query, keys_blk, preferred_element_type=jnp.fl...  17.6 us
    reduce_sum x4, other arithmetic, tile_step(): totals = totals * factor + jnp.sum(weight, axis=-1)  14.6 us
    dot_general x4, matrix products, tile_step(): jnp.einsum('hqk,khd->hqd', weight.astype(jnp.bfloat16), vals_blk, preferr...  12.6 us
    all_gather x1, waiting for transfers between devices, local(): piece = lax.all_gather(w_qkv, 'gx', axis=0, tiled=True)  12 us
  transfers between devices with their start and end apart: 8, of which 7 were waited for; matrix products, arithmetic and copies ran while one was open for 23% of the time, Pallas kernels for 0%

profile of v1, /device:TPU:0, one launch (start us, length us, event | category | flops | bytes accessed | tf_op | source)
XLA Modules:
  0.0 240.6 jit_solution(17509374633634083205)
XLA Ops:
  7.2 0.0 all-gather.7.cloned.1.call-start
  7.2 0.7 all-gather.7.cloned.1.call-update
  7.9 0.0 all-gather.9.cloned.1.call-start
  7.9 3.1 %collective-permute-start = (bf16[384,512]{1,0:T(8,128)(2,1)}, bf16[384,512]{1,0:T(8,128)(2,1)S(1)}, u32[]{:S(2)}, u32[]{:S(2)}) collective-permute-start(bf16[384,512]{1,0:T(8,128)(2,1)} %param.7), channel_id=1, source_target_pairs={{0,1},{1,2},{2,3},{3,0},{4,5},{5,6},{6,7},{7,4},{8,9},{9,10},{10,1... | collective-permute-start | bytes 1179656 | tf_op jit(solution)/shard_map/ppermute | solution.py:42
  11.0 0.8 reduce-window.9
  11.9 0.7 bitcast_subtract_fusion
  12.5 9.9 %collective-permute-done = bf16[384,512]{1,0:T(8,128)(2,1)S(1)} collective-permute-done((bf16[384,512]{1,0:T(8,128)(2,1)}, bf16[384,512]{1,0:T(8,128)(2,1)S(1)}, u32[]{:S(2)}, u32[]{:S(2)}) %collective-permute-start) | collective-permute-done | bytes 393248 | tf_op jit(solution)/shard_map/ppermute | solution.py:42
  22.4 0.0 collective-permute-start.1
  22.4 0.1 select_reduce_fusion
  22.5 12.0 %collective-permute-done.1 = bf16[384,512]{1,0:T(8,128)(2,1)S(1)} collective-permute-done((bf16[384,512]{1,0:T(8,128)(2,1)S(1)}, bf16[384,512]{1,0:T(8,128)(2,1)S(1)}, u32[]{:S(2)}, u32[]{:S(2)}) %collective-permute-start.1) | collective-permute-done | bytes 393248 | tf_op jit(solution)/shard_map/ppermute | solution.py:42
  34.5 0.4 multiply_cosine_fusion
  35.0 0.2 broadcast_in_dim.92
  35.2 1.0 constant_dynamic-update-slice_fusion.3
  36.2 0.1 constant_dynamic-update-slice_fusion.2
  36.3 9.3 %collective-permute-done.2 = bf16[384,512]{1,0:T(8,128)(2,1)S(1)} collective-permute-done((bf16[384,512]{1,0:T(8,128)(2,1)S(1)}, bf16[384,512]{1,0:T(8,128)(2,1)S(1)}, u32[]{:S(2)}, u32[]{:S(2)}) %collective-permute-start.2) | collective-permute-done | bytes 393248 | tf_op jit(solution)/shard_map/ppermute | solution.py:42
  45.7 0.4 fusion.22
  46.1 0.0 copy-start.3
  46.1 12.0 %all-gather.7.cloned.1.call-done = bf16[2048,3,4,128]{3,2,1,0:T(4,128)(2,1)} async-done(((bf16[256,3,4,128]{3,2,1,0:T(4,128)(2,1)}), bf16[2048,3,4,128]{3,2,1,0:T(4,128)(2,1)}) %all-gather.7.cloned.1.call-update) | async-done | bytes 6291472 | tf_op jit(solution)/shard_map/all_gather | solution.py:46
  58.1 10.6 %copy.41 = bf16[2048,3,4,128]{0,3,2,1:T(8,128)(2,1)} copy(bf16[2048,3,4,128]{3,2,1,0:T(4,128)(2,1)} %all-gather.7.cloned.1.call-done) | data formatting | bytes 12582912 | tf_op jit(solution)/shard_map/reshape | solution.py:49
  68.7 5.7 %fusion.20 = f32[384,3,4,128]{0,3,2,1:T(8,128)S(1)} fusion(bf16[2048,3,4,128]{0,3,2,1:T(8,128)(2,1)} %copy.41, bf16[384,2048]{1,0:T(8,128)(2,1)S(1)} %constant_dynamic-update-slice_fusion, f32[2048]{0:T(1024)S(1)} %copy-done.3, f32[384]{0:T(512)S(1)} %add_rsqrt_fusion), kind=kOutput, calls=%fused_computation.25 | convolution fusion | flops 2419064832 | bytes 10233344 | tf_op jit(solution)/shard_map/dot_general | solution.py:48
  74.5 0.1 slice_bitcast_fusion
  74.6 0.2 subtract_convert_fusion
  74.8 1.2 copy-done.2
  75.9 0.8 pad_maximum_fusion
  76.7 0.0 all-gather.9.cloned.1.call-update
  76.8 0.0 all-gather.15.cloned.1.call-start
  76.8 1.9 slice.47
  78.7 0.0 all-gather.15.cloned.1.call-update
  78.8 0.0 all-gather.13.cloned.1.call-start
  78.8 0.5 all-gather.13.cloned.1.call-update
  79.3 0.0 all-gather.11.cloned.1.call-start
  79.5 0.2 copy.34
  79.7 30.0 %all-gather.9.cloned.1.call-done = bf16[3072,4,128]{0,2,1:T(8,128)(2,1)} async-done(((bf16[384,4,128]{0,2,1:T(8,128)(2,1)}), bf16[3072,4,128]{0,2,1:T(8,128)(2,1)}) %all-gather.9.cloned.1.call-update) | async-done | bytes 3145744 | tf_op jit(solution)/shard_map/all_gather | solution.py:88
  109.7 35.3 %all-gather.15.cloned.1.call-done = bf16[3072,1,4,128]{0,3,2,1:T(8,128)(2,1)} async-done(((bf16[384,1,4,128]{0,3,2,1:T(8,128)(2,1)}), bf16[3072,1,4,128]{0,3,2,1:T(8,128)(2,1)}) %all-gather.15.cloned.1.call-update) | async-done | bytes 3145744 | tf_op jit(solution)/shard_map/all_gather | solution.py:89
  145.0 46.8 %while.18 = (s32[]{:T(128)}, f32[4,384]{1,0:T(4,128)S(1)}, f32[4,384]{1,0:T(4,128)S(1)}, f32[4,384,128]{2,1,0:T(8,128)S(1)}, s32[384]{0:T(512)S(1)}, /*index=5*/...) while((s32[]{:T(128)}, f32[4,384]{1,0:T(4,128)S(1)}, ...), condition=%wide.region_6.7_spmd.clone, body=%wide.region_3.6_spmd.clone.sunk | while | flops 620798592 | bytes 37858016 | solution.py:99
  145.0 0.3 compare_and_fusion.2
  145.3 4.4 %fusion.42 = (f32[4,384]{1,0:T(4,128)S(1)}, f32[4,768,384]{2,1,0:T(8,128)}) fusion(pred[384,768]{0,1:T(8,128)(4,1)S(1)} %compare_and_fusion.2, bf16[384,4,128]{2,0,1:T(8,128)(2,1)S(1)} %get-tuple-element.368, bf16[3072,4,128]{0,2,1:T(8,128)(2,1)} %get-tuple-element.367, s32[]{:T(128)S(6)} %select_n.102), kind=kOutput, calls=%fused_computation.3.clone.1 | convolution fusion | flops 305527296 | bytes 6199300 | tf_op jit(solution)/shard_map/while/body/eval_jaxpr/qhd,khd->hqk/dot_general | solution.py:66
  149.8 3.7 %fusion.43 = f32[4,384]{1,0:T(4,128)S(1)} fusion(f32[4,768,384]{2,1,0:T(8,128)} %get-tuple-element.333, f32[4,384]{1,0:T(4,128)S(1)} %select_maximum_fusion.2, pred[384,768]{0,1:T(8,128)(4,1)S(1)} %compare_and_fusion.2), kind=kLoop, calls=%fused_computation.5.clone.1 | loop fusion | flops 5896704 | bytes 5025792 | tf_op jit(solution)/shard_map/while/body/eval_jaxpr/reduce_sum | solution.py:73
  153.4 0.1 copy-done
  153.6 3.2 %fusion.45 = f32[4,384,128]{2,1,0:T(8,128)S(1)} fusion(f32[4,768,384]{2,1,0:T(8,128)S(1)} %copy-done, f32[4,384]{1,0:T(4,128)S(1)} %select_maximum_fusion.2, pred[384,768]{0,1:T(8,128)(4,1)S(1)} %compare_and_fusion.2, f32[4,384,128]{2,1,0:T(8,128)S(1)} %get-tuple-element.352, bf16[3072,4,128]{0,2,1:T(8,128)(2,1)} %get-tuple-element.369, ...), kind=kOutput, calls=%fused_computation.8.clone.1 | convolution fusion | flops 308477952 | bytes 7385093 | tf_op jit(solution)/shard_map/while/body/eval_jaxpr/hqk,khd->hqd/dot_general | solution.py:74
  156.8 0.3 compare_and_fusion.2
  157.1 4.4 %fusion.42 = (f32[4,384]{1,0:T(4,128)S(1)}, f32[4,768,384]{2,1,0:T(8,128)}) fusion(pred[384,768]{0,1:T(8,128)(4,1)S(1)} %compare_and_fusion.2, bf16[384,4,128]{2,0,1:T(8,128)(2,1)S(1)} %get-tuple-element.368, bf16[3072,4,128]{0,2,1:T(8,128)(2,1)} %get-tuple-element.367, s32[]{:T(128)S(6)} %select_n.102), kind=kOutput, calls=%fused_computation.3.clone.1 | convolution fusion | flops 305527296 | bytes 6199300 | tf_op jit(solution)/shard_map/while/body/eval_jaxpr/qhd,khd->hqk/dot_general | solution.py:66
  161.5 3.7 %fusion.43 = f32[4,384]{1,0:T(4,128)S(1)} fusion(f32[4,768,384]{2,1,0:T(8,128)} %get-tuple-element.333, f32[4,384]{1,0:T(4,128)S(1)} %select_maximum_fusion.2, pred[384,768]{0,1:T(8,128)(4,1)S(1)} %compare_and_fusion.2), kind=kLoop, calls=%fused_computation.5.clone.1 | loop fusion | flops 5896704 | bytes 5025792 | tf_op jit(solution)/shard_map/while/body/eval_jaxpr/reduce_sum | solution.py:73
  165.2 0.1 copy-done
  165.3 3.1 %fusion.45 = f32[4,384,128]{2,1,0:T(8,128)S(1)} fusion(f32[4,768,384]{2,1,0:T(8,128)S(1)} %copy-done, f32[4,384]{1,0:T(4,128)S(1)} %select_maximum_fusion.2, pred[384,768]{0,1:T(8,128)(4,1)S(1)} %compare_and_fusion.2, f32[4,384,128]{2,1,0:T(8,128)S(1)} %get-tuple-element.352, bf16[3072,4,128]{0,2,1:T(8,128)(2,1)} %get-tuple-element.369, ...), kind=kOutput, calls=%fused_computation.8.clone.1 | convolution fusion | flops 308477952 | bytes 7385093 | tf_op jit(solution)/shard_map/while/body/eval_jaxpr/hqk,khd->hqd/dot_general | solution.py:74
  168.5 0.3 compare_and_fusion.2
  168.8 4.4 %fusion.42 = (f32[4,384]{1,0:T(4,128)S(1)}, f32[4,768,384]{2,1,0:T(8,128)}) fusion(pred[384,768]{0,1:T(8,128)(4,1)S(1)} %compare_and_fusion.2, bf16[384,4,128]{2,0,1:T(8,128)(2,1)S(1)} %get-tuple-element.368, bf16[3072,4,128]{0,2,1:T(8,128)(2,1)} %get-tuple-element.367, s32[]{:T(128)S(6)} %select_n.102), kind=kOutput, calls=%fused_computation.3.clone.1 | convolution fusion | flops 305527296 | bytes 6199300 | tf_op jit(solution)/shard_map/while/body/eval_jaxpr/qhd,khd->hqk/dot_general | solution.py:66
  173.2 3.7 %fusion.43 = f32[4,384]{1,0:T(4,128)S(1)} fusion(f32[4,768,384]{2,1,0:T(8,128)} %get-tuple-element.333, f32[4,384]{1,0:T(4,128)S(1)} %select_maximum_fusion.2, pred[384,768]{0,1:T(8,128)(4,1)S(1)} %compare_and_fusion.2), kind=kLoop, calls=%fused_computation.5.clone.1 | loop fusion | flops 5896704 | bytes 5025792 | tf_op jit(solution)/shard_map/while/body/eval_jaxpr/reduce_sum | solution.py:73
  176.9 0.1 copy-done
  177.0 3.1 %fusion.45 = f32[4,384,128]{2,1,0:T(8,128)S(1)} fusion(f32[4,768,384]{2,1,0:T(8,128)S(1)} %copy-done, f32[4,384]{1,0:T(4,128)S(1)} %select_maximum_fusion.2, pred[384,768]{0,1:T(8,128)(4,1)S(1)} %compare_and_fusion.2, f32[4,384,128]{2,1,0:T(8,128)S(1)} %get-tuple-element.352, bf16[3072,4,128]{0,2,1:T(8,128)(2,1)} %get-tuple-element.369, ...), kind=kOutput, calls=%fused_computation.8.clone.1 | convolution fusion | flops 308477952 | bytes 7385093 | tf_op jit(solution)/shard_map/while/body/eval_jaxpr/hqk,khd->hqd/dot_general | solution.py:74
  180.2 0.3 compare_and_fusion.2
  180.5 4.4 %fusion.42 = (f32[4,384]{1,0:T(4,128)S(1)}, f32[4,768,384]{2,1,0:T(8,128)}) fusion(pred[384,768]{0,1:T(8,128)(4,1)S(1)} %compare_and_fusion.2, bf16[384,4,128]{2,0,1:T(8,128)(2,1)S(1)} %get-tuple-element.368, bf16[3072,4,128]{0,2,1:T(8,128)(2,1)} %get-tuple-element.367, s32[]{:T(128)S(6)} %select_n.102), kind=kOutput, calls=%fused_computation.3.clone.1 | convolution fusion | flops 305527296 | bytes 6199300 | tf_op jit(solution)/shard_map/while/body/eval_jaxpr/qhd,khd->hqk/dot_general | solution.py:66
  184.9 3.7 %fusion.43 = f32[4,384]{1,0:T(4,128)S(1)} fusion(f32[4,768,384]{2,1,0:T(8,128)} %get-tuple-element.333, f32[4,384]{1,0:T(4,128)S(1)} %select_maximum_fusion.2, pred[384,768]{0,1:T(8,128)(4,1)S(1)} %compare_and_fusion.2), kind=kLoop, calls=%fused_computation.5.clone.1 | loop fusion | flops 5896704 | bytes 5025792 | tf_op jit(solution)/shard_map/while/body/eval_jaxpr/reduce_sum | solution.py:73
  188.6 0.1 copy-done
  188.7 3.1 %fusion.45 = f32[4,384,128]{2,1,0:T(8,128)S(1)} fusion(f32[4,768,384]{2,1,0:T(8,128)S(1)} %copy-done, f32[4,384]{1,0:T(4,128)S(1)} %select_maximum_fusion.2, pred[384,768]{0,1:T(8,128)(4,1)S(1)} %compare_and_fusion.2, f32[4,384,128]{2,1,0:T(8,128)S(1)} %get-tuple-element.352, bf16[3072,4,128]{0,2,1:T(8,128)(2,1)} %get-tuple-element.369, ...), kind=kOutput, calls=%fused_computation.8.clone.1 | convolution fusion | flops 308477952 | bytes 7385093 | tf_op jit(solution)/shard_map/while/body/eval_jaxpr/hqk,khd->hqd/dot_general | solution.py:74
  191.8 0.0 copy-start.1
  191.8 0.3 copy.36
  192.1 0.8 divide_convert_fusion
  192.9 0.0 all-gather.11.cloned.1.call-update
  193.0 1.0 copy.37
  193.9 1.2 slice_bitcast_fusion.2
  195.1 1.0 copy.38
  196.1 34.2 %all-gather.11.cloned.1.call-done = bf16[384,2048]{0,1:T(8,128)(2,1)} async-done(((bf16[384,512]{0,1:T(8,128)(2,1)}), bf16[384,2048]{0,1:T(8,128)(2,1)}) %all-gather.11.cloned.1.call-update) | async-done | bytes 1572880 | tf_op jit(solution)/shard_map/all_gather | solution.py:102
  230.2 3.8 %convolution_convert_fusion = bf16[384,512]{1,0:T(8,128)(2,1)} fusion(bf16[384,2048]{0,1:T(8,128)(2,1)} %all-gather.11.cloned.1.call-done, bf16[2048,512]{1,0:T(8,128)(2,1)} %all-gather.13.cloned.1.call-done), kind=kOutput, calls=%fused_computation.35 | convolution fusion | flops 805502976 | bytes 4063232 | tf_op jit(solution)/shard_map/dot_general | solution.py:104
  (39 shorter events, 0.3 us)
Async XLA Ops:
  7.2 51.0 %all-gather.7.cloned.1.call-start = ((), (), s32[]{:S(2)}) async-start(), calls=%async_computation | async-start | bytes 7077888 | tf_op jit(solution)/shard_map/all_gather | solution.py:46
  7.9 101.8 %all-gather.9.cloned.1.call-start = ((), (), s32[]{:S(2)}) async-start(), calls=%async_computation.1 | async-start | bytes 3538944 | tf_op jit(solution)/shard_map/all_gather | solution.py:88
  7.9 14.4 %collective-permute-start = (bf16[384,512]{1,0:T(8,128)(2,1)}, bf16[384,512]{1,0:T(8,128)(2,1)S(1)}, u32[]{:S(2)}, u32[]{:S(2)}) collective-permute-start(bf16[384,512]{1,0:T(8,128)(2,1)} %param.7), channel_id=1, source_target_pairs={{0,1},{1,2},{2,3},{3,0},{4,5},{5,6},{6,7},{7,4},{8,9},{9,10},{10,1... | collective-permute-start | bytes 1179656 | tf_op jit(solution)/shard_map/ppermute | solution.py:42
  22.4 12.1 %collective-permute-start.1 = (bf16[384,512]{1,0:T(8,128)(2,1)S(1)}, bf16[384,512]{1,0:T(8,128)(2,1)S(1)}, u32[]{:S(2)}, u32[]{:S(2)}) collective-permute-start(bf16[384,512]{1,0:T(8,128)(2,1)S(1)} %collective-permute-done), channel_id=1, source_target_pairs={{0,1},{1,2},{2,3},{3,0},{4,5},{5,6},{6,7},{7,4},{8,9},{9,10},{10,1... | collective-permute-start | bytes 1179656 | tf_op jit(solution)/shard_map/ppermute | solution.py:42
  34.5 11.2 %collective-permute-start.2 = (bf16[384,512]{1,0:T(8,128)(2,1)S(1)}, bf16[384,512]{1,0:T(8,128)(2,1)S(1)}, u32[]{:S(2)}, u32[]{:S(2)}) collective-permute-start(bf16[384,512]{1,0:T(8,128)(2,1)S(1)} %collective-permute-done.1), channel_id=1, source_target_pairs={{0,1},{1,2},{2,3},{3,0},{4,5},{5,6},{6,7},{7,4},{8,9},{9,10},{10,1... | collective-permute-start | bytes 1179656 | tf_op jit(solution)/shard_map/ppermute | solution.py:42
  46.1 22.6 %copy-start.3 = (f32[2048]{0:T(1024)S(1)}, f32[2048]{0:T(1024)}, u32[]{:S(2)}) copy-start(f32[2048]{0:T(1024)} %param.8) | copy-start | bytes 24580
  74.4 1.5 copy-start.2
  76.8 68.3 %all-gather.15.cloned.1.call-start = ((), (), s32[]{:S(2)}) async-start(), calls=%async_computation.4 | async-start | bytes 3538944 | tf_op jit(solution)/shard_map/all_gather | solution.py:89
  78.8 117.3 %all-gather.13.cloned.1.call-start = ((), (), s32[]{:S(2)}) async-start(), calls=%async_computation.3 | async-start | bytes 2359296 | tf_op jit(solution)/shard_map/all_gather | solution.py:105
  79.3 150.9 %all-gather.11.cloned.1.call-start = ((), (), s32[]{:S(2)}) async-start(), calls=%async_computation.2 | async-start | bytes 1966080 | tf_op jit(solution)/shard_map/all_gather | solution.py:102
  149.8 3.8 %copy-start = (f32[4,768,384]{2,1,0:T(8,128)S(1)}, f32[4,768,384]{2,1,0:T(8,128)}, u32[]{:S(2)}) copy-start(f32[4,768,384]{2,1,0:T(8,128)} %get-tuple-element.333) | copy-start | bytes 14155780 | tf_op jit(solution)/shard_map/while
  161.5 3.8 %copy-start = (f32[4,768,384]{2,1,0:T(8,128)S(1)}, f32[4,768,384]{2,1,0:T(8,128)}, u32[]{:S(2)}) copy-start(f32[4,768,384]{2,1,0:T(8,128)} %get-tuple-element.333) | copy-start | bytes 14155780 | tf_op jit(solution)/shard_map/while
  173.2 3.8 %copy-start = (f32[4,768,384]{2,1,0:T(8,128)S(1)}, f32[4,768,384]{2,1,0:T(8,128)}, u32[]{:S(2)}) copy-start(f32[4,768,384]{2,1,0:T(8,128)} %get-tuple-element.333) | copy-start | bytes 14155780 | tf_op jit(solution)/shard_map/while
  184.9 3.8 %copy-start = (f32[4,768,384]{2,1,0:T(8,128)S(1)}, f32[4,768,384]{2,1,0:T(8,128)}, u32[]{:S(2)}) copy-start(f32[4,768,384]{2,1,0:T(8,128)} %get-tuple-element.333) | copy-start | bytes 14155780 | tf_op jit(solution)/shard_map/while
  191.8 1.1 copy-start.1
Sparse Core Ops, SparseCore 0:
  9.9 48.2 all-gather.6
  76.9 32.8 all-gather.8
  112.2 32.8 all-gather.14
  146.8 27.8 all-gather.12
  193.1 37.1 all-gather.10
